TPU v7x, 32 devices: a whole 2x2x4 slice. The times are simulated.
32 devices in a mesh: section: 2 (over y), blk: 8 (over z, x), mp: 2 (over core).
Axes of the slice: x: 2, y: 2, z: 4, core: 2. Of those that a mesh axis runs over, the one named last changes fastest.
Arguments:
- queries: bfloat16 [2, 1024, 4096], P('section', 'blk', 'mp'), may hold values from -210 to 210
- encoder_states: bfloat16 [512, 2048], P(('blk', 'section', 'mp')), may hold values from -200 to 200
- norm_gain: float32 [2048], replicated, may hold values from 0.25 to 1.75
- kv_weight: bfloat16 [2, 2048, 2, 512], P('section', 'blk', None, 'mp'), may hold values from -0.125 to 0.125
- span_len: int32 [64], replicated, may hold values from 1 to 57, as said below
- span_owner: int32 [64], replicated, may hold values from 0 to 7, as said below
Outputs:
- attended: bfloat16 [2, 1024, 4096], P('section', 'blk', 'mp')
Inputs may be any that keep to these rules, and one draw needn't show every extreme that they name: `span_owner`: each span lies whole in the slots of one blk index; each blk index owns exactly 8 spans. `span_len`: the spans of one blk index hold at most 64 tokens together, exactly 64 for some blk index in every draw; all spans hold 288 tokens together; one span holds exactly 57 tokens in every draw.
All inputs are finite; a program needn't handle non-finite values.
Results may differ from a plain program's by a relative error of at most 0.0094.
Values may be sent and summed in bfloat16 or wider, within the bound.
No kernel may reach another device: no remote copies, remote signals or barrier semaphores. Data moves between devices by JAX's collectives and lax.ppermute only.
A program may use at most 64 MiB of HBM per device.

v0:
```python
import jax
import jax.numpy as jnp
from jax import lax
from jax.sharding import PartitionSpec as P

HEADS = 32
KVH = 4
HD = 128


def normalize(states, norm_gain):
    widened = states.astype(jnp.float32)
    factor = lax.rsqrt(jnp.mean(widened * widened, axis=-1, keepdims=True) + 1e-05)
    return (widened * factor * norm_gain).astype(jnp.bfloat16)


def slot_loads(span_len, span_owner, block_count):
    owners = span_owner[:, None] == jnp.arange(block_count, dtype=jnp.int32)[None, :]
    return jnp.sum(jnp.where(owners, span_len[:, None], 0), axis=0)


def live_slots(slot_load, row_count, capacity):
    slot_ids = jnp.arange(row_count, dtype=jnp.int32)
    holder = slot_ids // capacity
    picked = holder[:, None] == jnp.arange(slot_load.shape[0], dtype=jnp.int32)[None, :]
    holder_load = jnp.sum(jnp.where(picked, slot_load[None, :], 0), axis=1)
    return slot_ids % capacity < holder_load


def attend_block(state_now, query_grid, key_rows, value_rows, alive):
    running_max, denominator, numerator = state_now
    row_count = key_rows.shape[0]
    groups = query_grid.shape[1]
    head_size = query_grid.shape[3]
    key_grid = key_rows.reshape(row_count, groups, head_size)
    value_grid = value_rows.reshape(row_count, groups, head_size)
    scores = jnp.einsum(
        "qgjd,rgd->qgjr", query_grid, key_grid, preferred_element_type=jnp.float32
    ) * head_size ** (-0.5)
    scores = jnp.where(alive, scores, -1e30)
    new_max = jnp.maximum(running_max, jnp.max(scores, axis=-1))
    weights = jnp.where(alive, jnp.exp(scores - new_max[..., None]), 0.0)
    denominator = jnp.sum(weights, axis=-1)
    numerator = jnp.einsum(
        "qgjr,rgd->qgjd",
        weights.astype(jnp.bfloat16),
        value_grid,
        preferred_element_type=jnp.float32,
    )
    return (new_max, denominator, numerator)


def attend(state_now, query_grid, key_rows, value_rows, slot_load, capacity):
    row_count = key_rows.shape[0]
    alive = live_slots(slot_load, row_count, capacity)
    return attend_block(state_now, query_grid, key_rows, value_rows, alive)


def local(queries, encoder_states, norm_gain, kv_weight, span_len, span_owner):
    gathered = lax.all_gather(encoder_states, ("section", "mp"), axis=0, tiled=True)
    capacity = gathered.shape[0]
    normed = normalize(gathered, norm_gain)
    block_count = lax.axis_size("blk")
    slot_load = slot_loads(span_len, span_owner, block_count)
    group_width = kv_weight.shape[3]
    local_groups = group_width // HD
    group_size = HEADS // KVH
    query_rows = queries.shape[1]
    query_grid = queries[0].reshape(query_rows, local_groups, group_size, HD)
    start_state = (
        jnp.full((query_rows, local_groups, group_size), -1e30, jnp.float32),
        jnp.zeros((query_rows, local_groups, group_size), jnp.float32),
        jnp.zeros((query_rows, local_groups, group_size, HD), jnp.float32),
    )
    projected = jnp.einsum(
        "cr,rtk->ctk",
        normed,
        lax.all_gather(kv_weight, "blk", axis=1, tiled=True)[0],
        preferred_element_type=jnp.float32,
    )
    key_rows = projected[:, 0].astype(jnp.bfloat16)
    value_rows = projected[:, 1].astype(jnp.bfloat16)
    final_state = attend(
        start_state,
        query_grid,
        lax.all_gather(key_rows, "blk", axis=0, tiled=True),
        lax.all_gather(value_rows, "blk", axis=0, tiled=True),
        slot_load,
        capacity,
    )
    denominator = final_state[1]
    numerator = final_state[2]
    attended = (numerator / denominator[..., None]).astype(jnp.bfloat16)
    return attended.reshape(1, query_rows, local_groups * group_size * HD)


def solution(mesh):
    in_specs = (
        P("section", "blk", "mp"),
        P(("blk", "section", "mp"), None),
        P(),
        P("section", "blk", None, "mp"),
        P(),
        P(),
    )
    out_specs = P("section", "blk", "mp")
    return jax.shard_map(local, mesh=mesh, in_specs=in_specs, out_specs=out_specs, check_vma=False)
```

profile of v0, /device:TPU:0, one launch (start us, length us, event | category | flops | bytes accessed | tf_op | source)
XLA Modules:
  0.0 140.6 jit_solution(526181429607966376)
XLA Ops:
  6.5 0.0 all-gather.4.cloned.1.call-start
  6.5 1.7 %copy.13 = bf16[1,256,2,256]{3,1,2,0:T(8,128)(2,1)} copy(bf16[1,256,2,256]{3,2,1,0:T(2,128)(2,1)} %param.9) | data formatting | bytes 524288 | tf_op args[3]
  8.2 0.0 all-gather.4.cloned.1.call-update
  8.2 1.1 copy.25
  9.4 7.5 %all_gather.12 = bf16[64,2048]{1,0:T(8,128)(2,1)S(1)} all-gather(bf16[16,2048]{1,0:T(8,128)(2,1)} %param.7), channel_id=1, replica_groups=mesh['section'=2,'blk'=8,'mp'=2] {'section','mp'}, dimensions={0}, use_global_device_ids=true | all-gather | bytes 327680 | tf_op jit(solution)/shard_map/all_gather | solution.py:60
  16.9 0.8 select_reduce_fusion.1
  17.6 0.1 select_reduce_fusion
  17.7 0.2 fusion.18
  17.9 43.4 %all-gather.4.cloned.1.call-done = bf16[1,2048,2,256]{3,1,2,0:T(8,128)(2,1)} async-done(((bf16[1,256,2,256]{3,1,2,0:T(8,128)(2,1)}), bf16[1,2048,2,256]{3,1,2,0:T(8,128)(2,1)}) %all-gather.4.cloned.1.call-update) | async-done | bytes 2097168 | tf_op jit(solution)/shard_map/all_gather | solution.py:78
  61.3 2.1 %fusion.13 = bf16[64,2,256]{2,0,1:T(8,128)(2,1)S(1)} fusion(bf16[1,2048,2,256]{3,1,2,0:T(8,128)(2,1)} %all-gather.4.cloned.1.call-done, bf16[64,2048]{1,0:T(8,128)(2,1)S(1)} %all_gather.12, f32[2048]{0:T(1024)} %param.8, f32[64]{0:T(128)S(1)} %add_rsqrt_fusion), kind=kOutput, calls=%fused_computation.13 | convolution fusion | flops 134774784 | bytes 2433280 | tf_op jit(solution)/shard_map/cr,rtk->ctk/dot_general | solution.py:75
  63.5 30.8 %all-gather.1 = bf16[512,1,256]{2,0,1:T(8,128)(2,1)S(1)} all-gather(bf16[64,1,256]{2,0,1:T(8,128)(2,1)S(1)} %get-tuple-element.5), channel_id=3, replica_groups=mesh['section'=2,'blk'=8,'mp'=2] {'blk'}, dimensions={0}, use_global_device_ids=true | all-gather | bytes 294912 | tf_op jit(solution)/shard_map/all_gather | solution.py:86
  94.3 0.1 reshape.41
  94.4 2.7 %bitcast_reduce_fusion = (f32[128,2,8]{0,2,1:T(8,128)S(1)}, f32[2,512,128,8]{2,1,3,0:T(8,128)}) fusion(pred[512]{0:T(512)(128)(4,1)S(1)} %fusion.28, bf16[128,2,8,128]{3,2,1,0:T(8,128)(2,1)S(1)} %bitcast.42, bf16[512,2,128,1]{2,1,0,3:T(2,128)(2,1)S(1)} %bitcast.43), kind=kOutput, calls=%fused_computation.1 | convolution fusion | flops 271579136 | bytes 4989440 | tf_op jit(solution)/shard_map/qgjd,rgd->qgjr/dot_general | solution.py:37
  97.1 30.8 %all-gather = bf16[512,1,256]{2,0,1:T(8,128)(2,1)S(1)} all-gather(bf16[64,1,256]{2,0,1:T(8,128)(2,1)S(1)} %get-tuple-element.6), channel_id=2, replica_groups=mesh['section'=2,'blk'=8,'mp'=2] {'blk'}, dimensions={0}, use_global_device_ids=true | all-gather | bytes 294912 | tf_op jit(solution)/shard_map/all_gather | solution.py:87
  127.9 0.1 copy.22
  128.0 0.0 copy-start
  128.0 3.4 %fusion.2 = f32[128,2,8]{0,2,1:T(8,128)S(1)} fusion(f32[2,512,128,8]{2,1,3,0:T(8,128)} %get-tuple-element.8, f32[128,2,8]{0,2,1:T(8,128)S(1)} %broadcast_maximum_fusion, pred[512]{0:T(512)(128)(4,1)S(1)} %fusion.28), kind=kLoop, calls=%fused_computation.5 | loop fusion | flops 5240832 | bytes 4211200 | tf_op jit(solution)/shard_map/reduce_sum | solution.py:43
  131.5 0.0 copy-done
  131.5 1.3 divide_convert_fusion
  132.8 1.0 copy.18
  (5 shorter events, 0.0 us)
Async XLA Ops:
  6.5 54.8 %all-gather.4.cloned.1.call-start = ((), (), s32[]{:S(2)}) async-start(), calls=%async_computation | async-start | bytes 2359296 | tf_op jit(solution)/shard_map/all_gather | solution.py:78
  128.0 3.5 %copy-start = (f32[2,512,128,8]{2,1,3,0:T(8,128)S(1)}, f32[2,512,128,8]{2,1,3,0:T(8,128)}, u32[]{:S(2)}) copy-start(f32[2,512,128,8]{2,1,3,0:T(8,128)} %get-tuple-element.8) | copy-start | bytes 12582916
Sparse Core Ops, SparseCore 0:
  9.5 51.7 all-gather.3
where the time goes:
time: 141 us
  blocking collectives  69.1 us (49%)
  waiting for transfers between devices  43.4 us (31%)
  between operations  13.5 us (10%)
  matrix products  6.14 us (4%)
  other arithmetic  4.49 us (3%)
  local copies, waits for them, and re-layouts  4.05 us (3%)
    all_gather x1, waiting for transfers between devices, local(): lax.all_gather(kv_weight, 'blk', axis=1, tiled=True)[0]  43.4 us
    all_gather x1, blocking collectives, local(): lax.all_gather(key_rows, 'blk', axis=0, tiled=True)  30.8 us
    all_gather x1, blocking collectives, local(): lax.all_gather(value_rows, 'blk', axis=0, tiled=True)  30.8 us
    all_gather x1, blocking collectives, local(): lax.all_gather(encoder_states, ('section', 'mp'), axis=0, tiled=True)  7.46 us
    reduce_sum x1, other arithmetic, attend_block(): denominator = jnp.sum(weights, axis=-1)  3.44 us
    unnamed x4, local copies, waits for them, and re-layouts  2.83 us
  transfers between devices with their start and end apart: 1, of which 1 were waited for; matrix products, arithmetic and copies ran while one was open for 2% of the time, Pallas kernels for 0%

commit v1 on v0

--- a/solution.py
+++ b/solution.py
@@ -6,6 +6,20 @@
 HEADS = 32
 KVH = 4
 HD = 128
+
+
+def slices_make(payload, which_axis="blk"):
+    ledger = [payload]
+    parts_n = lax.axis_size(which_axis)
+    for p in range(1, parts_n):
+        ledger.append(
+            lax.ppermute(
+                ledger[p - 1], which_axis, [(s, (s - 1) % parts_n) for s in range(parts_n)]
+            )
+        )
+    everything = jnp.concatenate(ledger, 0)
+    lower = jnp.roll(everything, lax.axis_index(which_axis) * payload.shape[0], 0)
+    return lower
 
 
 def normalize(states, norm_gain):
@@ -83,7 +97,7 @@
     final_state = attend(
         start_state,
         query_grid,
-        lax.all_gather(key_rows, "blk", axis=0, tiled=True),
+        slices_make(key_rows),
         lax.all_gather(value_rows, "blk", axis=0, tiled=True),
         slot_load,
         capacity,

time: 141 us -> 144 us (1.021)
  blocking collectives: 69.1 us -> 38.3 us
  starting transfers between devices: 0.01 us -> 27.4 us
  waiting for transfers between devices: 43.4 us -> 54 us
  other arithmetic: 4.49 us -> 2.2 us
  matrix products: 6.14 us -> 4.49 us
    all_gather x1 -> x0, blocking collectives: 30.8 us -> none  [local(): lax.all_gather(key_rows, 'blk', axis=0, tiled=True)]
    ppermute x0 -> x7, starting transfers between devices: none -> 27.4 us  [slices_make(): lax.ppermute(ledger[p - 1], which_axis, [(s, (s - 1) % parts_n) for s in...]
    ppermute x0 -> x7, waiting for transfers between devices: none -> 10.6 us  [slices_make(): lax.ppermute(ledger[p - 1], which_axis, [(s, (s - 1) % parts_n) for s in...]
    reduce_sum x1, other arithmetic: 3.44 us -> 1.16 us  [attend_block(): denominator = jnp.sum(weights, axis=-1)]
    dot_general x1, matrix products: 2.74 us -> 1.09 us  [attend_block(): jnp.einsum('qgjd,rgd->qgjr', query_grid, key_grid, preferred_element_type...]
    unnamed x4 -> x17, local copies, waits for them, and re-layouts: 2.83 us -> 2.88 us
  transfers between devices with their start and end apart: 1 -> 8, of which waited for: 1 -> 7; matrix products, arithmetic and copies ran while one was open for 2% -> 2% of each run, Pallas kernels for 0% -> 0%
where the time goes in v1:
time: 144 us
  waiting for transfers between devices  54 us (38%)
  blocking collectives  38.3 us (27%)
  starting transfers between devices  27.4 us (19%)
  between operations  13.6 us (9%)
  matrix products  4.49 us (3%)
  local copies, waits for them, and re-layouts  4.21 us (3%)
  other arithmetic  2.2 us (2%)
    all_gather x1, waiting for transfers between devices, local(): lax.all_gather(kv_weight, 'blk', axis=1, tiled=True)[0]  43.4 us
    all_gather x1, blocking collectives, local(): lax.all_gather(value_rows, 'blk', axis=0, tiled=True)  30.8 us
    ppermute x7, starting transfers between devices, slices_make(): lax.ppermute(ledger[p - 1], which_axis, [(s, (s - 1) % parts_n) for s in...  27.4 us
    ppermute x7, waiting for transfers between devices, slices_make(): lax.ppermute(ledger[p - 1], which_axis, [(s, (s - 1) % parts_n) for s in...  10.6 us
    all_gather x1, blocking collectives, local(): lax.all_gather(encoder_states, ('section', 'mp'), axis=0, tiled=True)  7.46 us
    unnamed x17, local copies, waits for them, and re-layouts  2.88 us
  transfers between devices with their start and end apart: 8, of which 7 were waited for; matrix products, arithmetic and copies ran while one was open for 2% of the time, Pallas kernels for 0%

profile of v1, /device:TPU:0, one launch (start us, length us, event | category | flops | bytes accessed | tf_op | source)
XLA Modules:
  0.0 144.2 jit_solution(16578353406024057037)
XLA Ops:
  6.5 0.0 all-gather.3.cloned.1.call-start
  6.5 1.7 %copy.19 = bf16[1,256,2,256]{3,1,2,0:T(8,128)(2,1)} copy(bf16[1,256,2,256]{3,2,1,0:T(2,128)(2,1)} %param.9) | data formatting | bytes 524288 | tf_op args[3]
  8.2 0.0 all-gather.3.cloned.1.call-update
  8.3 1.1 copy.32
  9.4 7.5 %all_gather.9 = bf16[64,2048]{1,0:T(8,128)(2,1)S(1)} all-gather(bf16[16,2048]{1,0:T(8,128)(2,1)} %param.7), channel_id=1, replica_groups=mesh['section'=2,'blk'=8,'mp'=2] {'section','mp'}, dimensions={0}, use_global_device_ids=true | all-gather | bytes 327680 | tf_op jit(solution)/shard_map/all_gather | solution.py:74
  16.9 0.8 select_reduce_fusion.1
  17.7 0.1 select_reduce_fusion
  17.8 0.2 fusion.18
  17.9 43.4 %all-gather.3.cloned.1.call-done = bf16[1,2048,2,256]{3,1,2,0:T(8,128)(2,1)} async-done(((bf16[1,256,2,256]{3,1,2,0:T(8,128)(2,1)}), bf16[1,2048,2,256]{3,1,2,0:T(8,128)(2,1)}) %all-gather.3.cloned.1.call-update) | async-done | bytes 2097168 | tf_op jit(solution)/shard_map/all_gather | solution.py:92
  61.3 2.1 %fusion.13 = bf16[64,2,256]{2,0,1:T(8,128)(2,1)S(1)} fusion(bf16[1,2048,2,256]{3,1,2,0:T(8,128)(2,1)} %all-gather.3.cloned.1.call-done, bf16[64,2048]{1,0:T(8,128)(2,1)S(1)} %all_gather.9, f32[2048]{0:T(1024)} %param.8, f32[64]{0:T(128)S(1)} %add_rsqrt_fusion), kind=kOutput, calls=%fused_computation.13 | convolution fusion | flops 134774784 | bytes 2433280 | tf_op jit(solution)/shard_map/cr,rtk->ctk/dot_general | solution.py:89
  63.5 1.9 %collective-permute-start = (bf16[64,256]{1,0:T(8,128)(2,1)S(1)}, bf16[64,256]{1,0:T(8,128)(2,1)S(1)}, u32[]{:S(2)}, u32[]{:S(2)}) collective-permute-start(bf16[64,256]{1,0:T(8,128)(2,1)S(1)} %get-tuple-element.5), channel_id=1, source_target_pairs={{0,14},{2,0},{4,2},{6,4},{8,6},{10,8},{12,10},{14,12},{1,15},{3,1}... | collective-permute-start | bytes 98312 | tf_op jit(solution)/shard_map/ppermute | solution.py:16
  65.4 30.8 %all-gather = bf16[512,1,256]{2,0,1:T(8,128)(2,1)S(1)} all-gather(bf16[64,1,256]{2,0,1:T(8,128)(2,1)S(1)} %get-tuple-element.6), channel_id=2, replica_groups=mesh['section'=2,'blk'=8,'mp'=2] {'blk'}, dimensions={0}, use_global_device_ids=true | all-gather | bytes 294912 | tf_op jit(solution)/shard_map/all_gather | solution.py:101
  96.2 0.1 copy.29
  96.4 0.0 collective-permute-done
  96.4 1.4 %collective-permute-start.1 = (bf16[64,256]{1,0:T(8,128)(2,1)S(1)}, bf16[64,256]{1,0:T(8,128)(2,1)S(1)}, u32[]{:S(2)}, u32[]{:S(2)}) collective-permute-start(bf16[64,256]{1,0:T(8,128)(2,1)S(1)} %collective-permute-done), channel_id=1, source_target_pairs={{0,14},{2,0},{4,2},{6,4},{8,6},{10,8},{12,10},{14,12},{1,15},{3,1}... | collective-permute-start | bytes 98312 | tf_op jit(solution)/shard_map/ppermute | solution.py:16
  97.8 2.6 %collective-permute-done.1 = bf16[64,256]{1,0:T(8,128)(2,1)S(1)} collective-permute-done((bf16[64,256]{1,0:T(8,128)(2,1)S(1)}, bf16[64,256]{1,0:T(8,128)(2,1)S(1)}, u32[]{:S(2)}, u32[]{:S(2)}) %collective-permute-start.1) | collective-permute-done | bytes 32800 | tf_op jit(solution)/shard_map/ppermute | solution.py:16
  100.4 4.0 %collective-permute-start.2 = (bf16[64,256]{1,0:T(8,128)(2,1)S(1)}, bf16[64,256]{1,0:T(8,128)(2,1)S(1)}, u32[]{:S(2)}, u32[]{:S(2)}) collective-permute-start(bf16[64,256]{1,0:T(8,128)(2,1)S(1)} %collective-permute-done.1), channel_id=1, source_target_pairs={{0,14},{2,0},{4,2},{6,4},{8,6},{10,8},{12,10},{14,12},{1,15},{3,1}... | collective-permute-start | bytes 98312 | tf_op jit(solution)/shard_map/ppermute | solution.py:16
  104.4 1.6 %collective-permute-done.2 = bf16[64,256]{1,0:T(8,128)(2,1)S(1)} collective-permute-done((bf16[64,256]{1,0:T(8,128)(2,1)S(1)}, bf16[64,256]{1,0:T(8,128)(2,1)S(1)}, u32[]{:S(2)}, u32[]{:S(2)}) %collective-permute-start.2) | collective-permute-done | bytes 32800 | tf_op jit(solution)/shard_map/ppermute | solution.py:16
  106.0 5.0 %collective-permute-start.3 = (bf16[64,256]{1,0:T(8,128)(2,1)S(1)}, bf16[64,256]{1,0:T(8,128)(2,1)S(1)}, u32[]{:S(2)}, u32[]{:S(2)}) collective-permute-start(bf16[64,256]{1,0:T(8,128)(2,1)S(1)} %collective-permute-done.2), channel_id=1, source_target_pairs={{0,14},{2,0},{4,2},{6,4},{8,6},{10,8},{12,10},{14,12},{1,15},{3,1}... | collective-permute-start | bytes 98312 | tf_op jit(solution)/shard_map/ppermute | solution.py:16
  111.0 1.6 %collective-permute-done.3 = bf16[64,256]{1,0:T(8,128)(2,1)S(1)} collective-permute-done((bf16[64,256]{1,0:T(8,128)(2,1)S(1)}, bf16[64,256]{1,0:T(8,128)(2,1)S(1)}, u32[]{:S(2)}, u32[]{:S(2)}) %collective-permute-start.3) | collective-permute-done | bytes 32800 | tf_op jit(solution)/shard_map/ppermute | solution.py:16
  112.6 5.0 %collective-permute-start.4 = (bf16[64,256]{1,0:T(8,128)(2,1)S(1)}, bf16[64,256]{1,0:T(8,128)(2,1)S(1)}, u32[]{:S(2)}, u32[]{:S(2)}) collective-permute-start(bf16[64,256]{1,0:T(8,128)(2,1)S(1)} %collective-permute-done.3), channel_id=1, source_target_pairs={{0,14},{2,0},{4,2},{6,4},{8,6},{10,8},{12,10},{14,12},{1,15},{3,1}... | collective-permute-start | bytes 98312 | tf_op jit(solution)/shard_map/ppermute | solution.py:16
  117.7 1.6 %collective-permute-done.4 = bf16[64,256]{1,0:T(8,128)(2,1)S(1)} collective-permute-done((bf16[64,256]{1,0:T(8,128)(2,1)S(1)}, bf16[64,256]{1,0:T(8,128)(2,1)S(1)}, u32[]{:S(2)}, u32[]{:S(2)}) %collective-permute-start.4) | collective-permute-done | bytes 32800 | tf_op jit(solution)/shard_map/ppermute | solution.py:16
  119.3 5.0 %collective-permute-start.5 = (bf16[64,256]{1,0:T(8,128)(2,1)S(1)}, bf16[64,256]{1,0:T(8,128)(2,1)S(1)}, u32[]{:S(2)}, u32[]{:S(2)}) collective-permute-start(bf16[64,256]{1,0:T(8,128)(2,1)S(1)} %collective-permute-done.4), channel_id=1, source_target_pairs={{0,14},{2,0},{4,2},{6,4},{8,6},{10,8},{12,10},{14,12},{1,15},{3,1}... | collective-permute-start | bytes 98312 | tf_op jit(solution)/shard_map/ppermute | solution.py:16
  124.3 1.6 %collective-permute-done.5 = bf16[64,256]{1,0:T(8,128)(2,1)S(1)} collective-permute-done((bf16[64,256]{1,0:T(8,128)(2,1)S(1)}, bf16[64,256]{1,0:T(8,128)(2,1)S(1)}, u32[]{:S(2)}, u32[]{:S(2)}) %collective-permute-start.5) | collective-permute-done | bytes 32800 | tf_op jit(solution)/shard_map/ppermute | solution.py:16
  125.9 5.0 %collective-permute-start.6 = (bf16[64,256]{1,0:T(8,128)(2,1)S(1)}, bf16[64,256]{1,0:T(8,128)(2,1)S(1)}, u32[]{:S(2)}, u32[]{:S(2)}) collective-permute-start(bf16[64,256]{1,0:T(8,128)(2,1)S(1)} %collective-permute-done.5), channel_id=1, source_target_pairs={{0,14},{2,0},{4,2},{6,4},{8,6},{10,8},{12,10},{14,12},{1,15},{3,1}... | collective-permute-start | bytes 98312 | tf_op jit(solution)/shard_map/ppermute | solution.py:16
  130.9 1.6 %collective-permute-done.6 = bf16[64,256]{1,0:T(8,128)(2,1)S(1)} collective-permute-done((bf16[64,256]{1,0:T(8,128)(2,1)S(1)}, bf16[64,256]{1,0:T(8,128)(2,1)S(1)}, u32[]{:S(2)}, u32[]{:S(2)}) %collective-permute-start.6) | collective-permute-done | bytes 32800 | tf_op jit(solution)/shard_map/ppermute | solution.py:16
  132.6 0.1 copy.20
  132.7 1.1 bitcast_reduce_fusion
  133.9 1.2 fusion.2
  135.0 1.3 divide_convert_fusion
  136.3 1.0 copy.25
  (22 shorter events, 0.1 us)
Async XLA Ops:
  6.5 54.8 %all-gather.3.cloned.1.call-start = ((), (), s32[]{:S(2)}) async-start(), calls=%async_computation | async-start | bytes 2359296 | tf_op jit(solution)/shard_map/all_gather | solution.py:92
  63.5 32.9 %collective-permute-start = (bf16[64,256]{1,0:T(8,128)(2,1)S(1)}, bf16[64,256]{1,0:T(8,128)(2,1)S(1)}, u32[]{:S(2)}, u32[]{:S(2)}) collective-permute-start(bf16[64,256]{1,0:T(8,128)(2,1)S(1)} %get-tuple-element.5), channel_id=1, source_target_pairs={{0,14},{2,0},{4,2},{6,4},{8,6},{10,8},{12,10},{14,12},{1,15},{3,1}... | collective-permute-start | bytes 98312 | tf_op jit(solution)/shard_map/ppermute | solution.py:16
  96.4 4.0 %collective-permute-start.1 = (bf16[64,256]{1,0:T(8,128)(2,1)S(1)}, bf16[64,256]{1,0:T(8,128)(2,1)S(1)}, u32[]{:S(2)}, u32[]{:S(2)}) collective-permute-start(bf16[64,256]{1,0:T(8,128)(2,1)S(1)} %collective-permute-done), channel_id=1, source_target_pairs={{0,14},{2,0},{4,2},{6,4},{8,6},{10,8},{12,10},{14,12},{1,15},{3,1}... | collective-permute-start | bytes 98312 | tf_op jit(solution)/shard_map/ppermute | solution.py:16
  100.4 5.6 %collective-permute-start.2 = (bf16[64,256]{1,0:T(8,128)(2,1)S(1)}, bf16[64,256]{1,0:T(8,128)(2,1)S(1)}, u32[]{:S(2)}, u32[]{:S(2)}) collective-permute-start(bf16[64,256]{1,0:T(8,128)(2,1)S(1)} %collective-permute-done.1), channel_id=1, source_target_pairs={{0,14},{2,0},{4,2},{6,4},{8,6},{10,8},{12,10},{14,12},{1,15},{3,1}... | collective-permute-start | bytes 98312 | tf_op jit(solution)/shard_map/ppermute | solution.py:16
  106.0 6.6 %collective-permute-start.3 = (bf16[64,256]{1,0:T(8,128)(2,1)S(1)}, bf16[64,256]{1,0:T(8,128)(2,1)S(1)}, u32[]{:S(2)}, u32[]{:S(2)}) collective-permute-start(bf16[64,256]{1,0:T(8,128)(2,1)S(1)} %collective-permute-done.2), channel_id=1, source_target_pairs={{0,14},{2,0},{4,2},{6,4},{8,6},{10,8},{12,10},{14,12},{1,15},{3,1}... | collective-permute-start | bytes 98312 | tf_op jit(solution)/shard_map/ppermute | solution.py:16
  112.6 6.6 %collective-permute-start.4 = (bf16[64,256]{1,0:T(8,128)(2,1)S(1)}, bf16[64,256]{1,0:T(8,128)(2,1)S(1)}, u32[]{:S(2)}, u32[]{:S(2)}) collective-permute-start(bf16[64,256]{1,0:T(8,128)(2,1)S(1)} %collective-permute-done.3), channel_id=1, source_target_pairs={{0,14},{2,0},{4,2},{6,4},{8,6},{10,8},{12,10},{14,12},{1,15},{3,1}... | collective-permute-start | bytes 98312 | tf_op jit(solution)/shard_map/ppermute | solution.py:16
  119.3 6.6 %collective-permute-start.5 = (bf16[64,256]{1,0:T(8,128)(2,1)S(1)}, bf16[64,256]{1,0:T(8,128)(2,1)S(1)}, u32[]{:S(2)}, u32[]{:S(2)}) collective-permute-start(bf16[64,256]{1,0:T(8,128)(2,1)S(1)} %collective-permute-done.4), channel_id=1, source_target_pairs={{0,14},{2,0},{4,2},{6,4},{8,6},{10,8},{12,10},{14,12},{1,15},{3,1}... | collective-permute-start | bytes 98312 | tf_op jit(solution)/shard_map/ppermute | solution.py:16
  125.9 6.6 %collective-permute-start.6 = (bf16[64,256]{1,0:T(8,128)(2,1)S(1)}, bf16[64,256]{1,0:T(8,128)(2,1)S(1)}, u32[]{:S(2)}, u32[]{:S(2)}) collective-permute-start(bf16[64,256]{1,0:T(8,128)(2,1)S(1)} %collective-permute-done.5), channel_id=1, source_target_pairs={{0,14},{2,0},{4,2},{6,4},{8,6},{10,8},{12,10},{14,12},{1,15},{3,1}... | collective-permute-start | bytes 98312 | tf_op jit(solution)/shard_map/ppermute | solution.py:16
Sparse Core Ops, SparseCore 0:
  9.5 51.7 all-gather.2
